TPU v7x, 512 devices: a whole 4x8x8 slice. The times are simulated.
512 devices in a mesh: row: 32 (over y, z_hi, core), col: 16 (over x, z_lo).
Axes of the slice: x: 4, y: 8, z: 8 (z_hi: 2, z_lo: 4; z = z_hi * 4 + z_lo), core: 2. Of those that a mesh axis runs over, the one named last changes fastest.
Arguments:
- traces: bfloat16 [2048, 64, 512], P(('row', 'col')), may hold values from -6 to 6
- live_flags: int32 [2048], P(('row', 'col')), may hold values 0 or 1
Outputs:
- correlations: bfloat16 [2048, 2048, 128], P('row', 'col')
Inputs may be any that keep to these rules, and one draw needn't show every extreme that they name: `live_flags`: 1 marks a working channel.
All inputs are finite; a program needn't handle non-finite values. No bound on the sum of `live_flags` on one device may be relied on, other than what follows from the above.
Results may differ from a plain program's by a relative error of at most 0.0058.
Values may be sent and summed in bfloat16 or wider, within the bound.
No kernel may reach another device: no remote copies, remote signals or barrier semaphores. Data moves between devices by JAX's collectives and lax.ppermute only.
A program may use at most 64 MiB of HBM per device.

v0:
```python
import math
import jax
import jax.numpy as jnp
from jax import lax
from jax.sharding import PartitionSpec as P

F = 256
LAGS = 128
SAMP = 512
NW = 64


def make_tables():
    samples = jnp.arange(SAMP, dtype=jnp.int32)
    bins = jnp.arange(F, dtype=jnp.int32)
    phase = samples[:, None] * bins[None, :] % SAMP
    angle = 2.0 * math.pi * phase.astype(jnp.float32) / SAMP
    forward = jnp.concatenate([jnp.cos(angle), -jnp.sin(angle)], axis=1)
    taper = 0.5 - 0.5 * jnp.cos(2.0 * math.pi * samples.astype(jnp.float32) / SAMP)
    near = (jnp.abs(bins[:, None] - bins[None, :]) <= 4).astype(jnp.float32)
    counts = jnp.sum(near, axis=0)
    lagval = jnp.arange(LAGS, dtype=jnp.int32) - LAGS // 2
    lphase = bins[:, None] * lagval[None, :] % SAMP
    langle = 2.0 * math.pi * lphase.astype(jnp.float32) / SAMP
    inverse = jnp.concatenate([jnp.cos(langle), -jnp.sin(langle)], axis=0).astype(jnp.bfloat16)
    return (forward, taper, near, counts, inverse)


def whiten(traces, live_flags, forward, taper, near, counts):
    chans = traces.shape[0]
    tapered = traces.astype(jnp.float32) * taper
    spectra = jnp.dot(tapered.reshape(-1, SAMP), forward, precision=lax.Precision.HIGHEST)
    real_part = spectra[:, :F]
    imag_part = spectra[:, F:]
    power = real_part * real_part + imag_part * imag_part
    smooth = jnp.dot(power, near, precision=lax.Precision.HIGHEST) / counts
    level = jnp.mean(power, axis=1, keepdims=True)
    scale = 1.0 / jnp.sqrt(smooth + 0.05 * level + 1e-06)
    alive = jnp.repeat(live_flags.astype(jnp.float32), NW)[:, None]
    white = jnp.concatenate([real_part * scale, imag_part * scale], axis=1) * alive
    white = white.reshape(chans, NW, 2, F)
    white = jnp.transpose(white, (3, 0, 2, 1)).reshape(F, chans, 2 * NW)
    return white.astype(jnp.bfloat16)


def cross_terms(first, second):
    half = first.shape[-1] // 2
    turned = jnp.concatenate([first[..., half:], -first[..., :half]], axis=2)
    cross_re = jnp.einsum("fik,fjk->fij", first, second, preferred_element_type=jnp.float32)
    cross_im = jnp.einsum("fik,fjk->fij", turned, second, preferred_element_type=jnp.float32)
    return (cross_re, cross_im)


def lag_block(cross_re, cross_im, inverse, low, high):
    stacked = (jnp.concatenate([cross_re, cross_im], axis=0) / math.sqrt(NW)).astype(jnp.bfloat16)
    table = jnp.concatenate([inverse[low:high], inverse[F + low : F + high]], axis=0)
    return lax.dot_general(
        stacked, table, (((0,), (0,)), ((), ())), preferred_element_type=jnp.float32
    )


def on_device(traces, live_flags):
    forward, taper, near, counts, inverse = make_tables()
    white = whiten(traces, live_flags, forward, taper, near, counts)
    per_dev = white.shape[1]
    width = F // 4
    first = lax.all_gather(white, "col", axis=1, tiled=True)
    second = lax.all_gather(white, "row", axis=1, tiled=True)
    pairs = (first, second)
    rows = pairs[0].shape[1]
    cols = pairs[1].shape[1]
    corr = jnp.zeros((rows, cols, LAGS), jnp.float32)
    for block in range(4):
        low = block * width
        high = low + width
        cross_re = None
        cross_im = None
        first, second = pairs
        part_re, part_im = cross_terms(first[low:high], second[low:high])
        cross_re = part_re
        cross_im = part_im
        corr = corr + lag_block(cross_re, cross_im, inverse, low, high)
    corr = corr / math.sqrt(F)
    n_col = lax.axis_size("col")
    chan_i = lax.axis_index("row") * rows + jnp.arange(rows, dtype=jnp.int32)
    local_j = jnp.arange(cols, dtype=jnp.int32)
    chan_j = (local_j // per_dev * n_col + lax.axis_index("col")) * per_dev + local_j % per_dev
    same = chan_i[:, None] == chan_j[None, :]
    corr = jnp.where(same[:, :, None], 0.0, corr)
    return corr.astype(jnp.bfloat16)


def solution(mesh):
    in_specs = (P(("row", "col"), None, None), P(("row", "col")))
    out_specs = P("row", "col", None)
    return jax.shard_map(
        on_device, mesh=mesh, in_specs=in_specs, out_specs=out_specs, check_vma=False
    )
```

profile of v0, /device:TPU:1, one launch (start us, length us, event | category | flops | bytes accessed | tf_op | source)
XLA Modules:
  0.0 307.1 jit_solution(10770554908488322001)
XLA Ops:
  6.6 2.1 sine_negate_fusion
  9.7 1.1 fusion.30
  14.1 108.5 %all-gather.3.cloned.1.call-done = bf16[256,64,128]{2,0,1:T(8,128)(2,1)} async-done(((bf16[256,4,128]{2,0,1:T(8,128)(2,1)}), bf16[256,64,128]{2,0,1:T(8,128)(2,1)}) %all-gather.3.cloned.1.call-update) | async-done | bytes 4194320 | tf_op jit(solution)/shard_map/all_gather | solution.py:67
  122.6 4.4 %fusion.90 = (bf16[64,64,64]{2,0,1:T(8,128)(2,1)S(1)}, bf16[64,64,64]{2,0,1:T(8,128)(2,1)S(1)}, bf16[64,64,64]{2,0,1:T(8,128)(2,1)S(1)}, bf16[64,64,64]{2,0,1:T(...) fusion(bf16[256,64,128]{2,0,1:T(8,128)(2,1)} %all-gather.3.clon, ...), kind=kLoop, calls=%fused_computation.131 | loop fusion | bytes 8388608 | tf_op jit(solution)/shard_map/slice | solution.py:48
  127.0 1.7 copy.65
  128.6 1.7 copy.57
  131.7 1.8 copy_negate_fusion.1
  133.4 1.8 copy_negate_fusion.3
  135.2 1.8 copy_negate_fusion.2
  137.9 2.7 fusion.89
  140.6 117.0 %all-gather.5.cloned.1.call-done = bf16[256,128,128]{2,0,1:T(8,128)(2,1)} async-done(((bf16[256,4,128]{2,0,1:T(8,128)(2,1)}), bf16[256,128,128]{2,0,1:T(8,128)(2,1)}) %all-gather.5.cloned.1.call-update) | async-done | bytes 8388624 | tf_op jit(solution)/shard_map/all_gather | solution.py:68
  257.6 4.7 %fusion.88 = (bf16[64,128,128]{2,0,1:T(8,128)(2,1)S(1)}, bf16[64,128,128]{2,0,1:T(8,128)(2,1)S(1)}, bf16[64,128,128]{2,0,1:T(8,128)(2,1)S(1)}, bf16[64,128,128]{2,0,1:T(8,128)(2,1)S(1)}) fusion(bf16[256,128,128]{2,0,1:T(8,128)(2,1)} %all-gather.5.cloned.1.call-done), kind=kLoop, calls=%fused_computation.129 | loop fusion | bytes 16777216 | tf_op jit(solution)/shard_map/slice | solution.py:79
  262.3 2.3 fusion.17
  264.7 2.3 fusion.15
  268.2 2.3 fusion.25
  270.6 2.3 fusion.23
  274.1 2.5 fusion.21
  276.7 2.3 fusion.19
  280.2 2.3 fusion.13
  282.5 2.3 fusion.11
  285.5 2.5 fusion.5
  288.0 2.8 fusion.9
  290.7 2.5 fusion.7
  293.3 6.8 %select_convert_fusion = bf16[64,128,128]{2,1,0:T(8,128)(2,1)} fusion(f32[64,128,128]{2,1,0:T(8,128)S(1)} %fusion.5, f32[64,128,128]{2,1,0:T(8,128)S(1)} %fusion.9, f32[64,128,128]{2,1,0:T(8,128)S(1)} %fusion.7, bf16[128,64,128]{2,1,0:T(8,128)(2,1)S(1)} %fusion.3, pred[64,128]{1,0:T(8,128)(4,1)S(1)} %broadcast_compare_fusion, ...), kind=kOutput, calls=%fused_computation.8 | convolution fusion | flops 274792448 | bytes 16818176 | tf_op jit(solution)/shard_map/dot_general | solution.py:57
  (50 shorter events, 10.8 us)
Async XLA Ops:
  6.5 116.1 %all-gather.3.cloned.1.call-start = ((), (), s32[]{:S(2)}) async-start(), calls=%async_computation | async-start | bytes 4456448 | tf_op jit(solution)/shard_map/all_gather | solution.py:67
  10.9 0.8 copy-start.10
  12.7 244.9 %all-gather.5.cloned.1.call-start = ((), (), s32[]{:S(2)}) async-start(), calls=%async_computation.1 | async-start | bytes 8650752 | tf_op jit(solution)/shard_map/all_gather | solution.py:68
  135.2 2.7 copy-start
  257.6 4.7 %copy-start.9 = (bf16[64,64,128]{2,0,1:T(8,128)(2,1)S(1)}, bf16[64,64,128]{2,0,1:T(8,128)(2,1)}, u32[]{:S(2)}) copy-start(bf16[64,64,128]{2,0,1:T(8,128)(2,1)} %get-tuple-element.10) | copy-start | bytes 3145732
  262.3 2.4 copy-start.3
  262.3 2.4 copy-start.5
  267.0 1.2 copy-start.8
  268.2 2.3 copy-start.1
  268.2 2.3 copy-start.4
  272.9 1.2 copy-start.7
  274.1 2.5 copy-start.2
  279.0 1.2 copy-start.6
Sparse Core Ops, SparseCore 0:
  12.8 109.7 all-gather.2
  125.9 131.6 all-gather.4
where the time goes:
time: 311 us; the launch traced here: 307 us
  waiting for transfers between devices  226 us (73%)
  matrix products  34.8 us (11%)
  local copies, waits for them, and re-layouts  19.6 us (6%)
  between operations  13.9 us (4%)
  other arithmetic  12.6 us (4%)
    all_gather x1, waiting for transfers between devices, on_device(): second = lax.all_gather(white, 'row', axis=1, tiled=True)  117 us
    all_gather x1, waiting for transfers between devices, on_device(): first = lax.all_gather(white, 'col', axis=1, tiled=True)  108 us
    dot_general x4, matrix products, lag_block(): lax.dot_general(stacked, table, (((0,), (0,)), ((), ())), preferred_eleme...  14.6 us
    dot_general x4, matrix products, cross_terms(): jnp.einsum('fik,fjk->fij', first, second, preferred_element_type=jnp.floa...  9.54 us
    dot_general x4, matrix products, cross_terms(): jnp.einsum('fik,fjk->fij', turned, second, preferred_element_type=jnp.flo...  9.29 us
    slice x2, local copies, waits for them, and re-layouts, on_device(): part_re, part_im = cross_terms(first[low:high], second[low:high])  7.4 us
    unnamed x26, local copies, waits for them, and re-layouts  6.67 us
  transfers between devices with their start and end apart: 2, of which 2 were waited for; matrix products, arithmetic and copies ran while one was open for 6% of the time, Pallas kernels for 0%

commit v1 on v0

--- a/solution.py
+++ b/solution.py
@@ -65,7 +65,8 @@
     per_dev = white.shape[1]
     width = F // 4
     first = lax.all_gather(white, "col", axis=1, tiled=True)
-    second = lax.all_gather(white, "row", axis=1, tiled=True)
+    sent = jnp.stack([white] * lax.axis_size("row"))
+    second = jnp.concatenate(lax.all_to_all(sent, "row", 0, 0), axis=1)
     pairs = (first, second)
     rows = pairs[0].shape[1]
     cols = pairs[1].shape[1]

time: 311 us -> 409 us (1.32)
  the two profiles are of different devices: /device:TPU:1 before, /device:TPU:24 now
where the time goes in v1:
time: 409 us; the launch traced here: 404 us
  waiting for transfers between devices  301 us (74%)
  matrix products  34.7 us (8%)
  local copies, waits for them, and re-layouts  24.3 us (6%)
  starting transfers between devices  16.5 us (4%)
  between operations  14.1 us (3%)
  other arithmetic  12.6 us (3%)
    all_gather x1, waiting for transfers between devices, on_device(): first = lax.all_gather(white, 'col', axis=1, tiled=True)  301 us
    all_to_all x1, starting transfers between devices, on_device(): second = jnp.concatenate(lax.all_to_all(sent, 'row', 0, 0), axis=1)  16 us
    dot_general x4, matrix products, lag_block(): lax.dot_general(stacked, table, (((0,), (0,)), ((), ())), preferred_eleme...  14.6 us
    dot_general x4, matrix products, cross_terms(): jnp.einsum('fik,fjk->fij', first, second, preferred_element_type=jnp.floa...  9.54 us
    dot_general x4, matrix products, cross_terms(): jnp.einsum('fik,fjk->fij', turned, second, preferred_element_type=jnp.flo...  9.21 us
  transfers between devices with their start and end apart: 2, of which 1 were waited for; matrix products, arithmetic and copies ran while one was open for 5% of the time, Pallas kernels for 0%

profile of v1, /device:TPU:24, one launch (start us, length us, event | category | flops | bytes accessed | tf_op | source)
XLA Modules:
  0.0 403.5 jit_solution(5267969029552378314)
XLA Ops:
  6.6 2.1 sine_negate_fusion
  12.0 5.3 %stack.2 = bf16[32,256,4,128]{3,1,2,0:T(8,128)(2,1)} broadcast(bf16[256,4,128]{2,0,1:T(8,128)(2,1)S(1)} %copy.37), dimensions={1,2,3} | broadcast | bytes 8650752 | tf_op jit(solution)/shard_map/stack | solution.py:68
  17.3 16.0 %all-to-all-start = ((bf16[32,256,4,128]{3,1,2,0:T(8,128)(2,1)}), bf16[32,256,4,128]{3,1,2,0:T(8,128)(2,1)}, u32[]{:S(2)}, u32[]{:S(2)}) async-start(bf16[32,256,4,128]{3,1,2,0:T(8,128)(2,1)} %stack.2), calls=%async_computation | async-start | bytes 16777216 | tf_op jit(solution)/shard_map/all_to_all | solution.py:69
  34.7 301.1 %all-gather.2.cloned.1.call-done = bf16[256,64,128]{2,0,1:T(8,128)(2,1)} async-done(((bf16[256,4,128]{2,0,1:T(8,128)(2,1)}), bf16[256,64,128]{2,0,1:T(8,128)(2,1)}) %all-gather.2.cloned.1.call-update) | async-done | bytes 4194320 | tf_op jit(solution)/shard_map/all_gather | solution.py:67
  335.8 4.3 %fusion.90 = (bf16[64,64,64]{2,0,1:T(8,128)(2,1)S(1)}, bf16[64,64,64]{2,0,1:T(8,128)(2,1)S(1)}, bf16[64,64,64]{2,0,1:T(8,128)(2,1)S(1)}, bf16[64,64,64]{2,0,1:T(...) fusion(bf16[256,64,128]{2,0,1:T(8,128)(2,1)} %all-gather.2.clon, ...), kind=kLoop, calls=%fused_computation.131 | loop fusion | bytes 8388608 | tf_op jit(solution)/shard_map/slice | solution.py:48
  340.2 1.7 copy.71
  341.9 1.7 copy.65
  344.9 1.8 copy_negate_fusion.1
  346.7 1.8 copy_negate_fusion.3
  348.5 1.8 copy_negate_fusion.2
  351.1 2.6 fusion.89
  353.8 4.8 %fusion.88 = (bf16[64,32,4,128]{3,0,2,1:T(8,128)(2,1)S(1)}, bf16[64,32,4,128]{3,0,2,1:T(8,128)(2,1)S(1)}, bf16[64,32,4,128]{3,0,2,1:T(8,128)(2,1)S(1)}, bf16[64,32,4,128]{3,0,2,1:T(8,128)(2,1)S(1)}) fusion(bf16[256,32,4,128]{3,0,2,1:T(8,128)(2,1)} %bitcast.4), kind=kLoop, calls=%fused_computation.129 | loop fusion | bytes 16777216 | tf_op jit(solution)/shard_map/slice | solution.py:80
  358.6 2.3 fusion.17
  361.0 2.3 fusion.15
  364.5 2.3 fusion.25
  366.8 2.3 fusion.23
  370.3 2.5 fusion.21
  372.9 2.3 fusion.19
  376.4 2.3 fusion.13
  378.8 2.3 fusion.11
  381.7 2.5 fusion.5
  384.2 2.8 fusion.9
  386.9 2.5 fusion.7
  389.5 6.8 %select_convert_fusion = bf16[64,128,128]{2,1,0:T(8,128)(2,1)} fusion(f32[64,128,128]{2,1,0:T(8,128)S(1)} %fusion.5, f32[64,128,128]{2,1,0:T(8,128)S(1)} %fusion.9, f32[64,128,128]{2,1,0:T(8,128)S(1)} %fusion.7, bf16[128,64,128]{2,1,0:T(8,128)(2,1)S(1)} %fusion.3, pred[64,128]{1,0:T(8,128)(4,1)S(1)} %broadcast_compare_fusion, ...), kind=kOutput, calls=%fused_computation.8 | convolution fusion | flops 274792448 | bytes 16818176 | tf_op jit(solution)/shard_map/dot_general | solution.py:57
  (52 shorter events, 11.1 us)
Async XLA Ops:
  10.9 0.8 copy-start.11
  12.0 5.3 %copy-start.10 = (bf16[256,4,128]{2,0,1:T(8,128)(2,1)}, bf16[256,4,128]{2,0,1:T(8,128)(2,1)S(1)}, u32[]{:S(2)}) copy-start(bf16[256,4,128]{2,0,1:T(8,128)(2,1)S(1)} %copy.37) | copy-start | bytes 786436
  17.3 336.5 %all-to-all-start = ((bf16[32,256,4,128]{3,1,2,0:T(8,128)(2,1)}), bf16[32,256,4,128]{3,1,2,0:T(8,128)(2,1)}, u32[]{:S(2)}, u32[]{:S(2)}) async-start(bf16[32,256,4,128]{3,1,2,0:T(8,128)(2,1)} %stack.2), calls=%async_computation | async-start | bytes 16777216 | tf_op jit(solution)/shard_map/all_to_all | solution.py:69
  33.3 302.5 %all-gather.2.cloned.1.call-start = ((), (), s32[]{:S(2)}) async-start(), calls=%async_computation.1 | async-start | bytes 4456448 | tf_op jit(solution)/shard_map/all_gather | solution.py:67
  348.5 2.6 copy-start
  353.8 4.8 %copy-start.9 = (bf16[64,64,128]{2,0,1:T(8,128)(2,1)S(1)}, bf16[64,64,128]{2,0,1:T(8,128)(2,1)}, u32[]{:S(2)}) copy-start(bf16[64,64,128]{2,0,1:T(8,128)(2,1)} %get-tuple-element.10) | copy-start | bytes 3145732
  358.6 2.4 copy-start.3
  358.6 2.4 copy-start.5
  363.3 1.2 copy-start.8
  364.5 2.3 copy-start.1
  364.5 2.3 copy-start.4
  369.1 1.2 copy-start.7
  370.3 2.5 copy-start.2
  375.2 1.2 copy-start.6
Sparse Core Ops, SparseCore 0:
  36.2 299.5 all-gather.1
